TPU v7x, 32 devices: a whole 2x2x4 slice. The times are simulated.
32 devices in a mesh: groups: 2 (over y), cell: 4 (over z), sc: 4 (over x, core).
Axes of the slice: x: 2, y: 2, z: 4, core: 2. Of those that a mesh axis runs over, the one named last changes fastest.
Arguments:
- symbols: bfloat16 [32, 2, 32, 4096], P(('groups', 'cell'), None, None, 'sc'), parts along dimension 0, may hold values from -4 to 4
- precoders: bfloat16 [32, 64, 16, 128], P(('groups', 'cell'), 'sc'), parts along dimension 0, may hold values from -1 to 1
- plan: int32 [32], P(('groups', 'cell')), parts along dimension 0, may hold values 0 or 1
- own_channel: bfloat16 [32, 16, 64, 128], P(('groups', 'cell'), None, 'sc'), parts along dimension 0, may hold values from -0.5 to 0.5
- cross_channel: bfloat16 [32, 16, 4, 64, 128], P(('groups', 'cell'), None, None, 'sc'), parts along dimension 0, may hold values from -0.375 to 0.375
- neighbours: int32 [32, 4], P(('groups', 'cell')), parts along dimension 0, may hold values from 0 to 15, as said below
- noise: bfloat16 [32, 16, 2, 2, 4096], P(('groups', 'cell'), None, None, None, 'sc'), parts along dimension 0, may hold values from -2 to 2
Outputs:
- time_signal: bfloat16 [32, 16, 2, 2, 4096], P(('groups', 'cell'), 'sc'), parts along dimension 0
There are 2 independent parts, one for each index of `groups`. A program takes and returns all parts, laid end to end along the dimension named above; each array names one. Nothing has to cross between parts.
Inputs may be any that keep to these rules, and one draw needn't show every extreme that they name: `neighbours`: each cell's 4 entries are distinct cells other than itself, each within 4 cells of it along the cycle of all 16 cells, where cell 0 follows cell 16 - 1.
All inputs are finite; a program needn't handle non-finite values. No bound on the sum of `plan` on one device may be relied on, other than what follows from the above.
Results may differ from a plain program's by a relative error of at most 0.0057.
Values may be sent and summed in bfloat16 or wider, within the bound.
No kernel may reach another device: no remote copies, remote signals or barrier semaphores. Data moves between devices by JAX's collectives and lax.ppermute only.
A program may use at most 64 MiB of HBM per device.

v0:
```python
import math

import jax
import jax.numpy as jnp
from jax import lax
from jax.sharding import PartitionSpec as P


def with_halo(value, sides, width):
    for axis, dim in sides:
        size, length = (lax.axis_size(axis), value.shape[dim])
        up = [(i, (i + 1) % size) for i in range(size)]
        down = [(j, i) for i, j in up]
        last = lax.slice_in_dim(value, length - width, length, axis=dim)
        initial = lax.slice_in_dim(value, 0, width, axis=dim)
        before = lax.ppermute(last, axis, up)
        after = lax.ppermute(initial, axis, down)
        value = jnp.concatenate([before, value, after], axis=dim)
    return value


def precode(weights, data_streams):
    half = weights.shape[-1] // 2
    real_part = weights[..., :half]
    imag_part = weights[..., half:]
    upper = jnp.concatenate([real_part, imag_part], axis=-1)
    lower = jnp.concatenate([-imag_part, real_part], axis=-1)
    blocks = jnp.concatenate([upper, lower], axis=-2)
    cell_total, symbol_total, spatial_layer_count, subcarrier_total = data_streams.shape
    subband_total = weights.shape[1]
    grouped_values = data_streams.reshape(
        cell_total,
        symbol_total,
        spatial_layer_count,
        subband_total,
        subcarrier_total // subband_total,
    )
    output_values = jnp.einsum(
        "ctvbs,cbva->ctbsa", grouped_values, blocks, preferred_element_type=jnp.float32
    )
    return output_values.reshape(cell_total, symbol_total, subcarrier_total, -1).astype(
        jnp.bfloat16
    )


def receive(transmit_signal, channel_matrix):
    half = channel_matrix.shape[-1] // 2
    real_part = channel_matrix[..., :half]
    imag_part = channel_matrix[..., half:]
    to_real = jnp.concatenate([real_part, -imag_part], axis=-1)
    to_imag = jnp.concatenate([imag_part, real_part], axis=-1)
    blocks = jnp.stack([to_real, to_imag], axis=-1)
    cell_total, symbol_total, subcarrier_total, spatial_layers = transmit_signal.shape
    subband_total = channel_matrix.shape[2]
    grouped_values = transmit_signal.reshape(
        cell_total, symbol_total, subband_total, subcarrier_total // subband_total, spatial_layers
    )
    output_values = jnp.einsum(
        "ctbsa,cubaz->cutzbs", grouped_values, blocks, preferred_element_type=jnp.float32
    )
    return output_values.reshape(
        cell_total, channel_matrix.shape[1], symbol_total, 2, subcarrier_total
    )


def dft_table(length):
    positions = jnp.arange(length, dtype=jnp.int32)
    product_mod = positions[:, None] * positions[None, :] % length
    angle = 2.0 * math.pi / length * product_mod.astype(jnp.float32)
    cosine = jnp.cos(angle)
    sine = jnp.sin(angle)
    return jnp.concatenate(
        [jnp.concatenate([cosine, sine], axis=1), jnp.concatenate([-sine, cosine], axis=1)], axis=0
    )


def time_signal(freq_grid):
    leading = freq_grid.shape[:-2]
    length = freq_grid.shape[-1]
    inner = math.gcd(length, 128)
    outer = length // inner
    data = freq_grid.astype(jnp.float32).reshape((-1, 2 * outer, inner))
    section = jnp.einsum("bks,kj->bjs", data, dft_table(outer), precision=lax.Precision.HIGHEST)
    outer_pos = jnp.arange(outer, dtype=jnp.int32)
    inner_pos = jnp.arange(inner, dtype=jnp.int32)
    twist_mod = outer_pos[:, None] * inner_pos[None, :] % length
    twist_angle = 2.0 * math.pi / length * twist_mod.astype(jnp.float32)
    twist_cos = jnp.cos(twist_angle)
    twist_sin = jnp.sin(twist_angle)
    real_rows = section[:, :outer]
    imag_rows = section[:, outer:]
    turned_real = real_rows * twist_cos - imag_rows * twist_sin
    turned_imag = real_rows * twist_sin + imag_rows * twist_cos
    combined = jnp.concatenate([turned_real, turned_imag], axis=-1)
    finished = jnp.matmul(combined, dft_table(inner), precision=lax.Precision.HIGHEST)
    finished = finished.reshape((-1, outer, 2, inner)).transpose(0, 2, 3, 1)
    timed = finished.reshape(leading + (2, length)) * (1.0 / math.sqrt(length))
    return timed.astype(jnp.bfloat16)


def body(symbols, precoders, plan, own_channel, cross_channel, neighbours, noise):
    cell_block = symbols.shape[0]
    gated_symbols = symbols * plan.astype(jnp.bfloat16)[:, None, None, None]
    transmit_signal = precode(precoders, gated_symbols)
    extended = with_halo(transmit_signal, (("cell", 0),), cell_block)
    received = receive(transmit_signal, own_channel)
    first_cell = lax.axis_index("cell") * cell_block
    all_cells = cell_block * lax.axis_size("cell")
    rows_local = (neighbours - first_cell + cell_block) % all_cells
    for slot_index in range(neighbours.shape[1]):
        source = jnp.take(extended, rows_local[:, slot_index], axis=0)
        received = received + receive(source, cross_channel[:, :, slot_index])
    freq_grid = (received + noise.astype(jnp.float32)).astype(jnp.bfloat16)
    return time_signal(lax.all_to_all(freq_grid, "sc", split_axis=1, concat_axis=4, tiled=True))


def solution(mesh):
    in_specs = (
        P(("groups", "cell"), None, None, "sc"),
        P(("groups", "cell"), "sc", None, None),
        P(("groups", "cell")),
        P(("groups", "cell"), None, "sc", None),
        P(("groups", "cell"), None, None, "sc", None),
        P(("groups", "cell"), None),
        P(("groups", "cell"), None, None, None, "sc"),
    )
    out_specs = P(("groups", "cell"), "sc", None, None, None)
    return jax.shard_map(body, mesh=mesh, in_specs=in_specs, out_specs=out_specs, check_vma=False)
```

profile of v0, /device:TPU:1, one launch (start us, length us, event | category | flops | bytes accessed | tf_op | source)
XLA Modules:
  0.0 163.2 jit_solution(17947351078825250928)
XLA Ops:
  0.0 2.0 %slice_negate_fusion = (bf16[4,16,16,64]{3,2,1,0:T(8,128)(2,1)}, bf16[4,16,16,64]{3,2,1,0:T(8,128)(2,1)}) fusion(bf16[4,16,16,128]{3,2,1,0:T(8,128)(2,1)} %param.10), kind=kLoop, calls=%fused_computation.74 | loop fusion | flops 65536 | bytes 524288 | tf_op jit(solution)/shard_map/neg | solution.py:27
  4.5 2.0 %convolution_convert_fusion = bf16[4,16,128,2,64]{2,4,3,1,0:T(8,128)(2,1)S(1)} fusion(bf16[4,2,32,16,64]{4,3,2,1,0:T(8,128)(2,1)S(1)} %reshape.81, bf16[4,16,16,64]{3,2,1,0:T(8,128)(2,1)} %get-tuple-element.43, bf16[4,16,16,64]{3,2,1,0:T(8,128)(2,1)} %get-tuple-element.42, bf16[4,16,16,128]{3,2,1,0:T(8,128)(2,1)S(1)} %copy-done.3), kind=kOutput, calls=%fused_computation.20 | convolution fusion | flops 69730304 | bytes 3145728 | tf_op jit(solution)/shard_map/ctvbs,cbva->ctbsa/dot_general | solution.py:38
  6.4 1.6 %copy.49 = bf16[4,2,16,64,128]{4,3,2,1,0:T(8,128)(2,1)} copy(bf16[4,2,16,64,128]{4,3,1,2,0:T(8,128)(2,1)S(1)} %bitcast.115) | data formatting | bytes 4194304 | tf_op jit(solution)/shard_map/convert_element_type | solution.py:41
  8.1 2.1 %collective-permute-start = (bf16[4,2,1024,128]{3,2,1,0:T(8,128)(2,1)}, bf16[4,2,1024,128]{3,2,1,0:T(8,128)(2,1)}, u32[]{:S(2)}, u32[]{:S(2)}) collective-permute-start(bf16[4,2,1024,128]{3,2,1,0:T(8,128)(2,1)} %bitcast.18), channel_id=1, source_target_pairs={{0,4},{4,8},{8,12},{12,0},{1,5},{5,9},{9,13},{13,1},{2,6},{6,10},{... | collective-permute-start | bytes 6291464 | tf_op jit(solution)/shard_map/ppermute | solution.py:16
  10.2 2.0 %collective-permute-start.1 = (bf16[4,2,1024,128]{3,2,1,0:T(8,128)(2,1)}, bf16[4,2,1024,128]{3,2,1,0:T(8,128)(2,1)}, u32[]{:S(2)}, u32[]{:S(2)}) collective-permute-start(bf16[4,2,1024,128]{3,2,1,0:T(8,128)(2,1)} %bitcast.18), channel_id=1, source_target_pairs={{4,0},{8,4},{12,8},{0,12},{5,1},{9,5},{13,9},{1,13},{6,2},{10,6},{... | collective-permute-start | bytes 6291464 | tf_op jit(solution)/shard_map/ppermute | solution.py:17
  17.6 3.5 %fusion = f32[4,16,16,2,2,64]{5,2,4,3,1,0:T(8,128)} fusion(bf16[4,16,128,2,64]{2,4,3,1,0:T(8,128)(2,1)S(1)} %convolution_convert_fusion, bf16[4,16,16,128,1]{3,1,4,2,0:T(8,128)(2,1)S(1)} %get-tuple-element.27, bf16[4,16,16,128,1]{3,1,4,2,0:T(8,128)(2,1)S(1)} %get-tuple-element.26), kind=kOutput, calls=%fused_computation.5 | convolution fusion | flops 68157440 | bytes 3670016 | tf_op jit(solution)/shard_map/ctbsa,cubaz->cutzbs/dot_general | solution.py:58
  21.0 36.9 %collective-permute-done = bf16[4,2,1024,128]{3,2,1,0:T(8,128)(2,1)} collective-permute-done((bf16[4,2,1024,128]{3,2,1,0:T(8,128)(2,1)}, bf16[4,2,1024,128]{3,2,1,0:T(8,128)(2,1)}, u32[]{:S(2)}, u32[]{:S(2)}) %collective-permute-start) | collective-permute-done | bytes 2097184 | tf_op jit(solution)/shard_map/ppermute | solution.py:16
  57.9 44.5 %collective-permute-done.1 = bf16[4,2,1024,128]{3,2,1,0:T(8,128)(2,1)} collective-permute-done((bf16[4,2,1024,128]{3,2,1,0:T(8,128)(2,1)}, bf16[4,2,1024,128]{3,2,1,0:T(8,128)(2,1)}, u32[]{:S(2)}, u32[]{:S(2)}) %collective-permute-start.1) | collective-permute-done | bytes 2097184 | tf_op jit(solution)/shard_map/ppermute | solution.py:17
  102.4 6.5 %pad_maximum_fusion = bf16[12,2,1024,128]{3,2,1,0:T(8,128)(2,1)} fusion(bf16[4,2,1024,128]{3,2,1,0:T(8,128)(2,1)} %collective-permute-done.1, bf16[4,2,1024,128]{3,2,1,0:T(8,128)(2,1)} %bitcast.18, bf16[4,2,1024,128]{3,2,1,0:T(8,128)(2,1)} %collective-permute-done), kind=kLoop, calls=%fused_computation.4 | loop fusion | flops 6291456 | bytes 12582912 | tf_op jit(solution)/shard_map/concatenate | solution.py:18
  108.9 4.9 %gather_fusion = bf16[4,2,1024,128]{3,2,1,0:T(8,128)(2,1)} fusion(bf16[12,2,1024,128]{3,2,1,0:T(8,128)(2,1)} %pad_maximum_fusion, s32[1024]{0:T(1024)S(1)} %pad_clamp_fusion.3), kind=kCustom, calls=%fused_computation.clone | custom fusion | bytes 4194320 | tf_op jit(solution)/shard_map/jit(_take)/gather | solution.py:111
  113.8 4.9 %gather_fusion.1 = bf16[4,2,1024,128]{3,2,1,0:T(8,128)(2,1)} fusion(bf16[12,2,1024,128]{3,2,1,0:T(8,128)(2,1)} %pad_maximum_fusion, s32[1024]{0:T(1024)S(1)} %pad_clamp_fusion.2), kind=kCustom, calls=%fused_computation.1.clone | custom fusion | bytes 4194320 | tf_op jit(solution)/shard_map/jit(_take)/gather | solution.py:111
  118.8 5.0 %gather_fusion.2 = bf16[4,2,1024,128]{3,2,1,0:T(8,128)(2,1)} fusion(bf16[12,2,1024,128]{3,2,1,0:T(8,128)(2,1)} %pad_maximum_fusion, s32[1024]{0:T(1024)S(1)} %pad_clamp_fusion.1), kind=kCustom, calls=%fused_computation.2.clone | custom fusion | bytes 4194320 | tf_op jit(solution)/shard_map/jit(_take)/gather | solution.py:111
  123.8 3.7 %gather_fusion.3 = bf16[4,2,1024,128]{3,2,1,0:T(8,128)(2,1)S(1)} fusion(bf16[12,2,1024,128]{3,2,1,0:T(8,128)(2,1)} %pad_maximum_fusion, s32[1024]{0:T(1024)S(1)} %pad_clamp_fusion), kind=kCustom, calls=%fused_computation.3.clone | custom fusion | bytes 4194320 | tf_op jit(solution)/shard_map/jit(_take)/gather | solution.py:111
  127.5 2.0 %broadcast_select_fusion.3 = bf16[4,2,1024,128]{3,2,1,0:T(8,128)(2,1)S(1)} fusion(bf16[4,2,1024,128]{3,2,1,0:T(8,128)(2,1)} %gather_fusion, pred[4]{0:T(512)(128)(4,1)S(1)} %get-tuple-element.51), kind=kLoop, calls=%fused_computation.19 | loop fusion | flops 1048576 | bytes 4194308 | tf_op jit(solution)/shard_map/jit(_take)/select_n | solution.py:111
  130.0 1.3 copy-done.1
  131.9 2.1 %fusion.8 = f32[4,16,16,2,2,64]{5,2,4,3,1,0:T(8,128)S(1)} fusion(bf16[4,2,16,64,128,1]{4,3,2,1,0,5:T(8,128)(2,1)S(1)} %bitcast.120, bf16[4,16,16,128,1]{3,1,4,2,0:T(8,128)(2,1)S(1)} %get-tuple-element.22, bf16[4,16,16,128,1]{3,1,4,2,0:T(8,128)(2,1)S(1)} %get-tuple-element.21), kind=kOutput, calls=%fused_computation.13 | convolution fusion | flops 68157440 | bytes 3670016 | tf_op jit(solution)/shard_map/ctbsa,cubaz->cutzbs/dot_general | solution.py:58
  133.9 2.1 %fusion.6 = f32[4,16,16,2,2,64]{5,2,4,3,1,0:T(8,128)S(1)} fusion(bf16[4,2,16,64,128,1]{4,3,2,1,0,5:T(8,128)(2,1)S(1)} %bitcast.119, bf16[4,16,16,128,1]{3,1,4,2,0:T(8,128)(2,1)S(1)} %get-tuple-element.33, bf16[4,16,16,128,1]{3,1,4,2,0:T(8,128)(2,1)S(1)} %get-tuple-element.32), kind=kOutput, calls=%fused_computation.11 | convolution fusion | flops 68157440 | bytes 3670016 | tf_op jit(solution)/shard_map/ctbsa,cubaz->cutzbs/dot_general | solution.py:58
  136.1 2.1 %fusion.4 = f32[4,16,16,2,2,64]{5,2,4,3,1,0:T(8,128)S(1)} fusion(bf16[4,2,16,64,128,1]{4,3,2,1,0,5:T(8,128)(2,1)S(1)} %bitcast.118, bf16[4,16,16,128,1]{3,1,4,2,0:T(8,128)(2,1)S(1)} %copy-done.4, bf16[4,16,16,128,1]{3,1,4,2,0:T(8,128)(2,1)S(1)} %get-tuple-element.37), kind=kOutput, calls=%fused_computation.9 | convolution fusion | flops 68157440 | bytes 3670016 | tf_op jit(solution)/shard_map/ctbsa,cubaz->cutzbs/dot_general | solution.py:58
  138.2 2.1 %add_bitcast_fusion = f32[4,16,2,2,16,64]{5,1,2,3,4,0:T(8,128)S(1)} fusion(f32[4,16,16,2,2,64]{5,2,4,3,1,0:T(8,128)S(1)} %fusion.4, f32[4,16,16,2,2,64]{5,2,4,3,1,0:T(8,128)S(1)} %fusion.6, f32[4,16,16,2,2,64]{5,2,4,3,1,0:T(8,128)S(1)} %copy-done, f32[4,16,16,2,2,64]{5,2,4,3,1,0:T(8,128)S(1)} %fusion.8, bf16[4,2,16,64,128,1]{4,3,2,1,0,5:T(8,128)(2,1)S(1)} %bitcast.116, ...), kind=kOutput, calls=%fused_computation.15 | convolution fusion | flops 69206016 | bytes 7864320 | tf_op jit(solution)/shard_map/ctbsa,cubaz->cutzbs/dot_general | solution.py:58
  142.1 1.3 add_convert_fusion
  143.3 1.3 copy.62
  144.7 4.5 %all-to-all-start = ((bf16[4,16,2,2,1024]{4,3,2,0,1:T(2,128)(2,1)}), bf16[4,16,2,2,1024]{4,3,2,0,1:T(2,128)(2,1)S(1)}, u32[]{:S(2)}, u32[]{:S(2)}) async-start(bf16[4,16,2,2,1024]{4,3,2,0,1:T(2,128)(2,1)} %copy.62), calls=%async_computation | async-start | bytes 1048576 | tf_op jit(solution)/shard_map/all_to_all | solution.py:114
  149.9 7.1 %all-to-all-done = bf16[4,16,2,2,1024]{4,3,2,0,1:T(2,128)(2,1)S(1)} async-done(((bf16[4,16,2,2,1024]{4,3,2,0,1:T(2,128)(2,1)}), bf16[4,16,2,2,1024]{4,3,2,0,1:T(2,128)(2,1)S(1)}, u32[]{:S(2)}, u32[]{:S(2)}) %all-to-all-start) | async-done | bytes 524320 | tf_op jit(solution)/shard_map/all_to_all | solution.py:114
  160.5 2.7 %convert_element_type.79 = bf16[4,4,2,2,4096]{4,3,2,1,0:T(2,128)(2,1)} reshape(bf16[32,2,128,32]{3,2,1,0:T(8,128)(2,1)S(1)} %bitcast.117) | data formatting | bytes 1048576 | tf_op jit(solution)/shard_map/convert_element_type | solution.py:98
  (63 shorter events, 14.5 us)
Async XLA Ops:
  0.0 4.4 %copy-start.3 = (bf16[4,16,16,128]{3,2,1,0:T(8,128)(2,1)S(1)}, bf16[4,16,16,128]{3,2,1,0:T(8,128)(2,1)}, u32[]{:S(2)}) copy-start(bf16[4,16,16,128]{3,2,1,0:T(8,128)(2,1)} %param.10) | copy-start | bytes 786436
  6.4 5.9 %copy-start.9 = (s32[4,4]{1,0:T(4,128)S(1)}, s32[4,4]{1,0:T(4,128)}, u32[]{:S(2)}) copy-start(s32[4,4]{1,0:T(4,128)} %param.14) | copy-start | bytes 196
  6.4 6.2 %copy-start.7 = (bf16[4,16,4,16,128]{4,3,2,1,0:T(8,128)(2,1)S(1)}, bf16[4,16,4,16,128]{4,3,2,1,0:T(8,128)(2,1)}, u32[]{:S(2)}) copy-start(bf16[4,16,4,16,128]{4,3,2,1,0:T(8,128)(2,1)} %param.13) | copy-start | bytes 3145732
  8.1 49.8 %collective-permute-start = (bf16[4,2,1024,128]{3,2,1,0:T(8,128)(2,1)}, bf16[4,2,1024,128]{3,2,1,0:T(8,128)(2,1)}, u32[]{:S(2)}, u32[]{:S(2)}) collective-permute-start(bf16[4,2,1024,128]{3,2,1,0:T(8,128)(2,1)} %bitcast.18), channel_id=1, source_target_pairs={{0,4},{4,8},{8,12},{12,0},{1,5},{5,9},{9,13},{13,1},{2,6},{6,10},{... | collective-permute-start | bytes 6291464 | tf_op jit(solution)/shard_map/ppermute | solution.py:16
  10.2 92.2 %collective-permute-start.1 = (bf16[4,2,1024,128]{3,2,1,0:T(8,128)(2,1)}, bf16[4,2,1024,128]{3,2,1,0:T(8,128)(2,1)}, u32[]{:S(2)}, u32[]{:S(2)}) collective-permute-start(bf16[4,2,1024,128]{3,2,1,0:T(8,128)(2,1)} %bitcast.18), channel_id=1, source_target_pairs={{4,0},{8,4},{12,8},{0,12},{5,1},{9,5},{13,9},{1,13},{6,2},{10,6},{... | collective-permute-start | bytes 6291464 | tf_op jit(solution)/shard_map/ppermute | solution.py:17
  12.8 1.0 copy-start.8
  127.5 2.2 %copy-start.2 = (bf16[4,2,1024,128]{3,2,1,0:T(8,128)(2,1)S(1)}, bf16[4,2,1024,128]{3,2,1,0:T(8,128)(2,1)}, u32[]{:S(2)}) copy-start(bf16[4,2,1024,128]{3,2,1,0:T(8,128)(2,1)} %gather_fusion.1) | copy-start | bytes 6291460
  129.7 1.6 copy-start.1
  133.9 2.1 %copy-start.4 = (bf16[4,16,16,128,1]{3,1,4,2,0:T(8,128)(2,1)S(1)}, bf16[4,16,16,128,1]{3,1,4,2,0:T(8,128)(2,1)}, u32[]{:S(2)}) copy-start(bf16[4,16,16,128,1]{3,1,4,2,0:T(8,128)(2,1)} %get-tuple-element.38) | copy-start | bytes 786436
  136.0 2.1 %copy-start = (f32[4,16,16,2,2,64]{5,2,4,3,1,0:T(8,128)S(1)}, f32[4,16,16,2,2,64]{5,2,4,3,1,0:T(8,128)}, u32[]{:S(2)}) copy-start(f32[4,16,16,2,2,64]{5,2,4,3,1,0:T(8,128)} %fusion) | copy-start | bytes 3145732
  136.1 2.1 %copy-start.5 = (bf16[4,16,16,128,1]{3,1,4,2,0:T(8,128)(2,1)S(1)}, bf16[4,16,16,128,1]{3,1,4,2,0:T(8,128)(2,1)}, u32[]{:S(2)}) copy-start(bf16[4,16,16,128,1]{3,1,4,2,0:T(8,128)(2,1)} %get-tuple-element.16) | copy-start | bytes 786436
  136.1 2.1 %copy-start.6 = (bf16[4,16,16,128,1]{3,1,4,2,0:T(8,128)(2,1)S(1)}, bf16[4,16,16,128,1]{3,1,4,2,0:T(8,128)(2,1)}, u32[]{:S(2)}) copy-start(bf16[4,16,16,128,1]{3,1,4,2,0:T(8,128)(2,1)} %get-tuple-element.17) | copy-start | bytes 786436
  144.7 12.4 %all-to-all-start = ((bf16[4,16,2,2,1024]{4,3,2,0,1:T(2,128)(2,1)}), bf16[4,16,2,2,1024]{4,3,2,0,1:T(2,128)(2,1)S(1)}, u32[]{:S(2)}, u32[]{:S(2)}) async-start(bf16[4,16,2,2,1024]{4,3,2,0,1:T(2,128)(2,1)} %copy.62), calls=%async_computation | async-start | bytes 1048576 | tf_op jit(solution)/shard_map/all_to_all | solution.py:114
where the time goes:
time: 165 us; the launch traced here: 163 us
  waiting for transfers between devices  88.5 us (54%)
  local copies, waits for them, and re-layouts  31.3 us (19%)
  other arithmetic  18.9 us (11%)
  matrix products  15.4 us (9%)
  starting transfers between devices  8.64 us (5%)
    ppermute x1, waiting for transfers between devices, with_halo(): after = lax.ppermute(initial, axis, down)  44.5 us
    ppermute x1, waiting for transfers between devices, with_halo(): before = lax.ppermute(last, axis, up)  36.9 us
    gather x4, local copies, waits for them, and re-layouts, body(): source = jnp.take(extended, rows_local[:, slot_index], axis=0)  18.6 us
    dot_general x5, matrix products, receive(): jnp.einsum('ctbsa,cubaz->cutzbs', grouped_values, blocks, preferred_eleme...  11.8 us
    all_to_all x1, waiting for transfers between devices, body(): lax.all_to_all(freq_grid, 'sc', split_axis=1, concat_axis=4, tiled=True)  7.13 us
    concatenate x1, other arithmetic, with_halo(): value = jnp.concatenate([before, value, after], axis=dim)  6.51 us
    all_to_all x1, starting transfers between devices, body(): lax.all_to_all(freq_grid, 'sc', split_axis=1, concat_axis=4, tiled=True)  4.5 us
    convert_element_type x2, local copies, waits for them, and re-layouts, time_signal(): return timed.astype(jnp.bfloat16)  3.74 us
  transfers between devices with their start and end apart: 3, of which 3 were waited for; matrix products, arithmetic and copies ran while one was open for 5% of the time, Pallas kernels for 0%

commit v1 on v0

v1 whole, which is shorter than its diff:
```python
import functools
import math

import jax
import jax.numpy as jnp
import numpy as np
from jax import lax
from jax.experimental import pallas as pl
from jax.experimental.pallas import tpu as pltpu
from jax.sharding import PartitionSpec as P

LANES = 128
SMEM = pltpu.MemorySpace.SMEM
BF16, F32 = jnp.bfloat16, jnp.float32
NT = (((1,), (1,)), ((), ()))


def combined_channel(idx_ref, h, p, base, slots, cells, users):
    half = p.shape[-1] // 2
    wide = p.astype(F32)
    lane = lax.broadcasted_iota(jnp.int32, wide.shape[1:], 1)
    p0 = [jnp.where(lane < half, wide[n], -wide[n]) for n in range(cells)]
    p1 = [pltpu.roll(wide[n], half, 1) for n in range(cells)]
    rows = [r for n in range(cells) for r in (p0[n], -p1[n])] + [r for n in range(cells) for r in (p1[n], p0[n])]
    rhs = jnp.concatenate(rows, axis=0).astype(BF16)
    prod = lax.dot_general(h, rhs, NT, preferred_element_type=F32)
    width = prod.shape[1] // 2
    source = lax.broadcasted_iota(jnp.int32, (users, width), 1) // (width // cells)
    out = []
    for z in range(2):
        for c in range(cells):
            acc = jnp.zeros((users, width), F32)
            for k in range(slots):
                start = (k * cells + c) * users
                part = prod[start : start + users, z * width : (z + 1) * width]
                acc = jnp.where(source == idx_ref[c, k] - base, part, acc)
            out.append(acc)
    return jnp.concatenate(out, axis=0).astype(BF16)


def pick_subbands(res, per):
    rows = res.shape[0] // per
    lane = lax.broadcasted_iota(jnp.int32, (rows, LANES), 1) // (LANES // per)
    out = res[:rows]
    for i in range(1, per):
        out = jnp.where(lane == i, res[i * rows : (i + 1) * rows], out)
    return out


def own_kernel(slots, cells, users, idx_ref, h_ref, p_ref, s_ref, noise_ref, acc_ref):
    per = h_ref.shape[0]
    g = jnp.concatenate(
        [combined_channel(idx_ref, h_ref[i], p_ref[:, i], cells, slots, cells, users) for i in range(per)], axis=0
    )
    for t in range(acc_ref.shape[0]):
        res = jnp.dot(g, s_ref[t], preferred_element_type=F32)
        acc_ref[t, 0] = noise_ref[t, 0].astype(F32) + pick_subbands(res, per)


def remote_kernel(slots, cells, users, idx_ref, h_ref, a_ref, b_ref, g_ref):
    per = h_ref.shape[0]
    out = []
    for i in range(per):
        parts = [
            combined_channel(idx_ref, h_ref[i], ref[:, i], base, slots, cells, users)
            for ref, base in ((a_ref, 0), (b_ref, 2 * cells))
        ]
        out.append(jnp.concatenate(parts, axis=1))
    g_ref[0] = jnp.concatenate(out, axis=0)


def grid_kernel(per, cells, users, me_ref, g_ref, a_ref, b_ref, acc_ref, *refs):
    outs, y, tiles = refs[:-2], refs[-2], refs[-1]
    blocks, rows = acc_ref.shape[0], acc_ref.shape[1]
    for r in range(blocks):
        lanes = slice(r * LANES, (r + 1) * LANES)
        s = jnp.concatenate([a_ref[:, lanes], b_ref[:, lanes]], axis=0)
        res = jnp.dot(g_ref[r], s, preferred_element_type=F32)
        y[r * rows : (r + 1) * rows] = acc_ref[r] + pick_subbands(res, per)
    half = rows // 2
    for row in range(half):
        tile = [y[pl.ds(z * half + row, blocks, stride=rows), :] for z in range(2)]
        tiles[row % users, row // users] = jnp.concatenate(tile, axis=0).astype(BF16)
    count = len(outs)
    for d in range(count):
        group = lax.rem(me_ref[0] + d, count)
        outs[d][...] = tiles[pl.ds(group * (users // count), users // count)]


def time_kernel(me_ref, w1_ref, tw_ref, w2_ref, *refs):
    parts, out_ref = refs[:-1], refs[-1]
    seqs = parts[0].shape[0] * parts[0].shape[1]
    rows = tw_ref.shape[1]
    w1 = w1_ref[me_ref[0]]
    w2 = w2_ref[...]
    n2 = w2.shape[0] // 2
    per = LANES // rows
    batch = min(seqs, 2 * per)
    cells = parts[0].shape[1]
    for first in range(0, seqs, batch):
        data = jnp.concatenate(
            [jnp.concatenate([p[q // cells, q % cells] for p in parts], axis=0) for q in range(first, first + batch)], axis=1
        )
        both = jnp.dot(w1, data, preferred_element_type=F32)
        both = both[: 2 * rows] + both[2 * rows :]
        turned = []
        for q in range(batch):
            re = both[:rows, q * LANES : (q + 1) * LANES]
            im = both[rows:, q * LANES : (q + 1) * LANES]
            turned.append(
                jnp.concatenate([re * tw_ref[0] - im * tw_ref[1], re * tw_ref[1] + im * tw_ref[0]], axis=1)
            )
        turned = jnp.concatenate(turned, axis=0)
        high = turned.astype(BF16)
        low = (turned - high.astype(F32)).astype(BF16)
        prod = lax.dot_general(w2, high, NT, preferred_element_type=F32)
        prod = prod[:n2] + prod[n2:] + lax.dot_general(w2[:n2], low, NT, preferred_element_type=F32)
        for z in range(2):
            for q in range(batch):
                group, at = divmod(q, per)
                pieces = []
                for i in range(per):
                    top = z * LANES + i * rows
                    left = group * LANES + at * rows
                    pieces.append(prod[top : top + rows, left : left + rows])
                seq = first + q
                out_ref[seq % cells, seq // cells, z] = jnp.concatenate(pieces, axis=1).astype(BF16)


def rotation(angle):
    return np.block([[np.cos(angle), -np.sin(angle)], [np.sin(angle), np.cos(angle)]])


def split_rows(table):
    high = table.astype(jnp.bfloat16)
    low = (table - high.astype(np.float64)).astype(jnp.bfloat16)
    return np.concatenate([high, low], axis=0)


def tables(length, parts):
    rows = length // LANES
    local = rows // parts
    m = np.arange(rows)
    w1 = []
    for me in range(parts):
        order = np.concatenate([(me - d) % parts * local + np.arange(local) for d in range(parts)])
        angle = 2 * np.pi * (np.outer(m, order) % rows) / rows
        full = rotation(angle).reshape(2 * rows, 2, parts, local).transpose(0, 2, 1, 3).reshape(2 * rows, 2 * rows)
        w1.append(split_rows(full))
    lane = np.arange(LANES)
    angle = 2 * np.pi * (np.outer(m, lane) % length) / length
    twist = (np.stack([np.cos(angle), np.sin(angle)]) / math.sqrt(length)).astype(np.float32)
    per = LANES // rows
    order = np.arange(LANES).reshape(rows, per).T.reshape(-1)
    angle = 2 * np.pi * (np.outer(order, lane) % LANES) / LANES
    w2 = split_rows(rotation(angle))
    return np.stack(w1), twist, w2


def whole(shape):
    return pl.BlockSpec(shape, lambda *_: (0,) * len(shape))


def body(symbols, precoders, plan, own_channel, cross_channel, neighbours, noise):
    cells, times, streams, width = symbols.shape
    subbands, users, slots, ants = precoders.shape[1], own_channel.shape[1], cross_channel.shape[2], precoders.shape[3]
    blocks = width // LANES
    per = subbands // blocks
    parts = lax.axis_size("sc")
    ring = lax.axis_size("cell")
    length = width * parts
    rows = 2 * cells * users
    up = [(i, (i + 1) % ring) for i in range(ring)]
    down = [(j, i) for i, j in up]

    def both_ways(x):
        return lax.ppermute(x, "cell", up), lax.ppermute(x, "cell", down)

    p_before, p_after = both_ways(precoders)
    gated = symbols * plan.astype(BF16)[:, None, None, None]
    gated = gated.transpose(1, 0, 2, 3).reshape(times, cells * streams, width)
    halos = [both_ways(gated[t]) for t in range(times)]

    base = lax.axis_index("cell") * cells
    idx = (neighbours - base + cells) % (cells * ring)
    idx = jnp.concatenate([idx, cells + jnp.arange(cells, dtype=jnp.int32)[:, None]], axis=1)
    cross = cross_channel.transpose(3, 2, 0, 1, 4).reshape(subbands, slots * cells * users, ants)
    own = own_channel.transpose(2, 0, 1, 3).reshape(subbands, cells * users, ants)
    chan = jnp.concatenate([cross, own], axis=1)
    noise_rows = noise.reshape(cells, users, times, 2, blocks, LANES).transpose(2, 4, 3, 0, 1, 5)
    noise_rows = noise_rows.reshape(times, blocks, rows, LANES)
    me = lax.axis_index("sc").astype(jnp.int32)[None]

    smem = pl.BlockSpec(memory_space=SMEM)
    p_spec = pl.BlockSpec((cells, per) + precoders.shape[2:], lambda r: (0, r, 0, 0))
    acc = pl.pallas_call(
        functools.partial(own_kernel, slots + 1, cells, users),
        grid=(blocks,),
        in_specs=[
            smem,
            pl.BlockSpec((per, (slots + 1) * cells * users, ants), lambda r: (r, 0, 0)),
            p_spec,
            pl.BlockSpec((times, cells * streams, LANES), lambda r: (0, 0, r)),
            pl.BlockSpec((times, 1, rows, LANES), lambda r: (0, r, 0, 0)),
        ],
        out_specs=pl.BlockSpec((times, 1, rows, LANES), lambda r: (0, r, 0, 0)),
        out_shape=jax.ShapeDtypeStruct((times, blocks, rows, LANES), F32),
        name="own_cells",
        cost_estimate=pl.CostEstimate(flops=2_000_000_000, bytes_accessed=4_000_000, transcendentals=0),
    )(idx, chan, precoders, gated, noise_rows)
    comb = pl.pallas_call(
        functools.partial(remote_kernel, slots, cells, users),
        grid=(blocks,),
        in_specs=[smem, pl.BlockSpec((per, slots * cells * users, ants), lambda r: (r, 0, 0)), p_spec, p_spec],
        out_specs=pl.BlockSpec((1, per * rows, 2 * cells * streams), lambda r: (r, 0, 0)),
        out_shape=jax.ShapeDtypeStruct((blocks, per * rows, 2 * cells * streams), BF16),
        name="other_cells",
        cost_estimate=pl.CostEstimate(flops=2_000_000_000, bytes_accessed=4_000_000, transcendentals=0),
    )(idx, chan, p_before, p_after)

    w1, twist, w2 = (jnp.asarray(x) for x in tables(length, parts))
    share = users // parts
    done = []
    for t in range(times):
        tile = (share, cells, 2 * blocks, LANES)
        sent = pl.pallas_call(
            functools.partial(grid_kernel, per, cells, users),
            in_specs=[smem] + [whole(x.shape) for x in (comb, *halos[t], acc[t])],
            out_specs=[whole(tile)] * parts,
            out_shape=[jax.ShapeDtypeStruct(tile, BF16)] * parts,
            grid=(1,),
            scratch_shapes=[
                pltpu.VMEM((blocks * rows, LANES), F32),
                pltpu.VMEM((users, cells, 2 * blocks, LANES), BF16),
            ],
            name="grid",
            cost_estimate=pl.CostEstimate(flops=1_000_000_000, bytes_accessed=3_000_000, transcendentals=0),
        )(me, comb, *halos[t], acc[t])
        got = [
            lax.ppermute(sent[d], "sc", [(i, (i + d) % parts) for i in range(parts)]) if d else sent[0] for d in range(parts)
        ]
        shape = (cells, share, 2, length // LANES, LANES)
        done.append(
            pl.pallas_call(
                time_kernel,
                in_specs=[smem] + [whole(x.shape) for x in (w1, twist, w2, *got)],
                out_specs=whole(shape),
                out_shape=jax.ShapeDtypeStruct(shape, BF16),
                grid=(1,),
                name="time",
                cost_estimate=pl.CostEstimate(flops=1_000_000_000, bytes_accessed=2_000_000, transcendentals=0),
            )(me, w1, twist, w2, *got)
        )
    return jnp.stack(done, axis=2).reshape(cells, share, times, 2, length)


def solution(mesh):
    in_specs = (
        P(("groups", "cell"), None, None, "sc"),
        P(("groups", "cell"), "sc", None, None),
        P(("groups", "cell")),
        P(("groups", "cell"), None, "sc", None),
        P(("groups", "cell"), None, None, "sc", None),
        P(("groups", "cell"), None),
        P(("groups", "cell"), None, None, None, "sc"),
    )
    out_specs = P(("groups", "cell"), "sc", None, None, None)
    return jax.shard_map(body, mesh=mesh, in_specs=in_specs, out_specs=out_specs, check_vma=False)
```

time: 165 us -> 58.3 us (0.35)
  waiting for transfers between devices: 88.5 us -> 0.03 us
  Pallas kernels: 0 us -> 25.1 us
  local copies, waits for them, and re-layouts: 31.3 us -> 9.61 us
  matrix products: 15.4 us -> 0 us
  other arithmetic: 18.9 us -> 5.11 us
  starting transfers between devices: 8.64 us -> 17.7 us
    ppermute x2 -> x12, waiting for transfers between devices: 81.4 us -> 0.03 us  [the longest x6 0.02 us: body(): lax.ppermute(sent[d], 'sc', [(i, (i + d) % parts) for i in range(parts)])]
    pallas_call x0 -> x6, Pallas kernels: none -> 25.1 us  [the longest x1 7.3 us: body(): pl.pallas_call(functools.partial(own_kernel, slots + 1, cells, users), gr...]
    gather x4 -> x0, local copies, waits for them, and re-layouts: 18.6 us -> none  [body(): source = jnp.take(extended, rows_local[:, slot_index], axis=0)]
    dot_general x8 -> x0, matrix products: 15.4 us -> none  [the longest x5 11.8 us: receive(): jnp.einsum('ctbsa,cubaz->cutzbs', grouped_values, blocks, preferred_eleme...]
    ppermute x2 -> x12, starting transfers between devices: 4.14 us -> 17.7 us  [the longest x6 10.7 us: both_ways(): return (lax.ppermute(x, 'cell', up), lax.ppermute(x, 'cell', down))]
    all_to_all x1 -> x0, waiting for transfers between devices: 7.13 us -> none  [body(): lax.all_to_all(freq_grid, 'sc', split_axis=1, concat_axis=4, tiled=True)]
    convert_element_type x4 -> x0, local copies, waits for them, and re-layouts: 6.71 us -> none  [the longest x2 3.74 us: time_signal(): return timed.astype(jnp.bfloat16)]
    concatenate x1 -> x2, other arithmetic: 6.51 us -> 1.81 us  [the longest x1 1.18 us: body(): chan = jnp.concatenate([cross, own], axis=1)]
  transfers between devices with their start and end apart: 3 -> 12, of which waited for: 3 -> 0; matrix products, arithmetic and copies ran while one was open for 5% -> 17% of each run, Pallas kernels for 0% -> 39%
where the time goes in v1:
time: 58.3 us; the launch traced here: 57.6 us
  Pallas kernels  25.1 us (43%)
  starting transfers between devices  17.7 us (30%)
  local copies, waits for them, and re-layouts  9.61 us (16%)
  other arithmetic  5.11 us (9%)
    ppermute x6, starting transfers between devices, both_ways(): return (lax.ppermute(x, 'cell', up), lax.ppermute(x, 'cell', down))  10.7 us
    pallas_call x1, Pallas kernels, body(): pl.pallas_call(functools.partial(own_kernel, slots + 1, cells, users), gr...  7.3 us
    ppermute x6, starting transfers between devices, body(): lax.ppermute(sent[d], 'sc', [(i, (i + d) % parts) for i in range(parts)])  6.94 us
    pallas_call x1, Pallas kernels, body(): pl.pallas_call(functools.partial(remote_kernel, slots, cells, users), gri...  6.67 us
    pallas_call x2, Pallas kernels, body(): pl.pallas_call(functools.partial(grid_kernel, per, cells, users), in_spec...  5.94 us
    pallas_call x2, Pallas kernels, body(): pl.pallas_call(time_kernel, in_specs=[smem] + [whole(x.shape) for x in (w...  5.17 us
    unnamed x22, local copies, waits for them, and re-layouts  2.34 us
    squeeze x1, local copies, waits for them, and re-layouts, body(): acc[t]  2.27 us
  transfers between devices with their start and end apart: 12, of which 0 were waited for; matrix products, arithmetic and copies ran while one was open for 17% of the time, Pallas kernels for 39%

profile of v1, /device:TPU:1, one launch (start us, length us, event | category | flops | bytes accessed | tf_op | source)
XLA Modules:
  0.0 57.6 jit_solution(17358222676084538946)
XLA Ops:
  0.0 2.1 %collective-permute-start = (bf16[4,16,16,128]{3,2,1,0:T(8,128)(2,1)}, bf16[4,16,16,128]{3,2,1,0:T(8,128)(2,1)}, u32[]{:S(2)}, u32[]{:S(2)}) collective-permute-start(bf16[4,16,16,128]{3,2,1,0:T(8,128)(2,1)} %p_ref.1), channel_id=1, source_target_pairs={{0,4},{4,8},{8,12},{12,0},{1,5},{5,9},{9,13},{13,1},{2,6},{6,10},{... | collective-permute-start | bytes 786440 | tf_op jit(solution)/shard_map/ppermute | solution.py:177
  2.1 2.0 %collective-permute-start.1 = (bf16[4,16,16,128]{3,2,1,0:T(8,128)(2,1)}, bf16[4,16,16,128]{3,2,1,0:T(8,128)(2,1)}, u32[]{:S(2)}, u32[]{:S(2)}) collective-permute-start(bf16[4,16,16,128]{3,2,1,0:T(8,128)(2,1)} %p_ref.1), channel_id=1, source_target_pairs={{4,0},{8,4},{12,8},{0,12},{5,1},{9,5},{13,9},{1,13},{6,2},{10,6},{... | collective-permute-start | bytes 786440 | tf_op jit(solution)/shard_map/ppermute | solution.py:177
  4.8 1.1 %multiply_bitcast_fusion = bf16[2,4,32,1024]{3,2,0,1:T(8,128)(2,1)S(1)} fusion(bf16[4,2,32,1024]{3,2,1,0:T(8,128)(2,1)} %param.10, bf16[4]{0:T(256)(128)(2,1)S(1)} %convert_element_type.3), kind=kLoop, calls=%fused_computation.4 | loop fusion | flops 262144 | bytes 1048584 | tf_op jit(solution)/shard_map/transpose | solution.py:181
  6.1 3.2 %collective-permute-start.3 = (bf16[128,1024]{1,0:T(8,128)(2,1)S(1)}, bf16[128,1024]{1,0:T(8,128)(2,1)}, u32[]{:S(2)}, u32[]{:S(2)}) collective-permute-start(bf16[128,1024]{1,0:T(8,128)(2,1)S(1)} %bitcast.34), channel_id=1, source_target_pairs={{4,0},{8,4},{12,8},{0,12},{5,1},{9,5},{13,9},{1,13},{6,2},{10,6},{... | collective-permute-start | bytes 786440 | tf_op jit(solution)/shard_map/ppermute | solution.py:177
  9.3 0.8 %copy.13 = bf16[2,4,32,1024]{3,2,1,0:T(8,128)(2,1)} copy(bf16[2,4,32,1024]{3,2,0,1:T(8,128)(2,1)S(1)} %multiply_bitcast_fusion) | data formatting | bytes 1048576 | tf_op jit(solution)/shard_map/transpose | solution.py:181
  10.2 0.7 %copy.11 = bf16[16,4,4,16,128]{4,3,2,1,0:T(8,128)(2,1)S(1)} copy(bf16[16,4,4,16,128]{4,0,1,3,2:T(8,128)(2,1)S(1)} %bitcast.25) | data formatting | bytes 2097152 | tf_op jit(solution)/shard_map/transpose | solution.py:187
  11.6 1.0 %copy.14 = bf16[4,16,2,2,8,128]{5,1,0,3,4,2:T(8,128)(2,1)} copy(bf16[4,16,2,2,8,128]{5,4,3,2,1,0:T(8,128)(2,1)S(1)} %reshape.36) | data formatting | bytes 1048576 | tf_op jit(solution)/shard_map/reshape | solution.py:190
  13.3 1.2 %pad_maximum_fusion.h_ref = bf16[16,320,128]{2,1,0:T(8,128)(2,1)} fusion(bf16[16,64,128]{2,1,0:T(8,128)(2,1)S(1)} %bitcast.24, bf16[16,256,128]{2,1,0:T(8,128)(2,1)S(1)} %bitcast.23), kind=kLoop, calls=%fused_computation | loop fusion | flops 2621440 | bytes 2621440 | tf_op jit(solution)/shard_map/concatenate | solution.py:189
  14.5 7.3 %own_cells.1 = f32[2,8,128,128]{3,2,1,0:T(8,128)} custom-call(s32[4,5]{1,0:T(4,128)} %pad_add_fusion.idx_ref, bf16[16,320,128]{2,1,0:T(8,128)(2,1)} %pad_maximum_fusion.h_ref, bf16[4,16,16,128]{3,2,1,0:T(8,128)(2,1)} %p_ref.1, bf16[2,128,1024]{2,1,0:T(8,128)(2,1)} %bitcast.28, bf16[2,8,128,128]{3,2,1,0:T(8,128)(2,1)} %bitcast.29), custom_call_target="tpu_custom_call" | custom-call | flops 2000000000 | bytes 4000000 | tf_op jit(solution)/shard_map/own_cells/pallas_call | solution.py:196
  21.8 2.3 %slice_bitcast_fusion.1 = (f32[8,128,128]{2,1,0:T(8,128)}, f32[8,128,128]{2,1,0:T(8,128)}) fusion(f32[2,8,128,128]{3,2,1,0:T(8,128)} %own_cells.1), kind=kLoop, calls=%fused_computation.2 | loop fusion | bytes 2097152 | tf_op jit(solution)/shard_map/squeeze | solution.py:238
  24.1 3.3 %collective-permute-start.8 = (bf16[128,1024]{1,0:T(8,128)(2,1)S(1)}, bf16[128,1024]{1,0:T(8,128)(2,1)S(1)}, u32[]{:S(2)}, u32[]{:S(2)}) collective-permute-start(bf16[128,1024]{1,0:T(8,128)(2,1)S(1)} %bitcast.32), channel_id=1, source_target_pairs={{4,0},{8,4},{12,8},{0,12},{5,1},{9,5},{13,9},{1,13},{6,2},{10,6},{... | collective-permute-start | bytes 786440 | tf_op jit(solution)/shard_map/ppermute | solution.py:177
  27.3 6.7 %other_cells.1.g_ref = bf16[8,256,256]{2,1,0:T(8,128)(2,1)} custom-call(s32[4,5]{1,0:T(4,128)} %pad_add_fusion.idx_ref, bf16[16,320,128]{2,1,0:T(8,128)(2,1)} %pad_maximum_fusion.h_ref, bf16[4,16,16,128]{3,2,1,0:T(8,128)(2,1)} %collective-permute-done.a_ref, bf16[4,16,16,128]{3,2,1,0:T(8,128)(2,1)} %collective-permute-done.1.b_ref), custom_call_target="tpu_custom_call" | custom-call | flops 2000000000 | bytes 4000000 | tf_op jit(solution)/shard_map/other_cells/pallas_call | solution.py:211
  34.0 3.0 %grid.2 = (bf16[4,4,16,128]{3,2,1,0:T(8,128)(2,1)}, bf16[4,4,16,128]{3,2,1,0:T(8,128)(2,1)}, bf16[4,4,16,128]{3,2,1,0:T(8,128)(2,1)}, bf16[4,4,16,128]{3,2,1,0:T(8,128)(2,1)}) custom-call(s32[1]{0:T(128)} %bitcast.me_ref, bf16[8,256,256]{2,1,0:T(8,128)(2,1)} %other_cells.1.g_ref, bf16[128,1024]{1,0:T(8,128)(2,1)} %collective-permute-done.2.a_ref, ...), custom_call_target="tpu_custom_call" | custom-call | flops 1000000000 | bytes 3000000 | tf_op jit(solution)/shard_map/grid/pallas_call | solution.py:226
  37.0 3.4 %collective-permute-start.4 = (bf16[4,4,16,128]{3,2,1,0:T(8,128)(2,1)}, bf16[4,4,16,128]{3,2,1,0:T(8,128)(2,1)S(1)}, u32[]{:S(2)}, u32[]{:S(2)}) collective-permute-start(bf16[4,4,16,128]{3,2,1,0:T(8,128)(2,1)} %get-tuple-element.14), channel_id=1, source_target_pairs={{0,1},{1,2},{2,3},{3,0},{4,5},{5,6},{6,7},{7,4},{8,9},{9,10},{10,1... | collective-permute-start | bytes 196616 | tf_op jit(solution)/shard_map/ppermute | solution.py:240
  40.8 0.7 %copy-done.4 = bf16[128,1024]{1,0:T(8,128)(2,1)} copy-done((bf16[128,1024]{1,0:T(8,128)(2,1)}, bf16[128,1024]{1,0:T(8,128)(2,1)S(1)}, u32[]{:S(2)}) %copy-start.4) | copy-done | bytes 262168
  41.5 3.0 %grid.3 = (bf16[4,4,16,128]{3,2,1,0:T(8,128)(2,1)}, bf16[4,4,16,128]{3,2,1,0:T(8,128)(2,1)}, bf16[4,4,16,128]{3,2,1,0:T(8,128)(2,1)}, bf16[4,4,16,128]{3,2,1,0:T(8,128)(2,1)}) custom-call(s32[1]{0:T(128)} %bitcast.me_ref, bf16[8,256,256]{2,1,0:T(8,128)(2,1)} %other_cells.1.g_ref, bf16[128,1024]{1,0:T(8,128)(2,1)} %collective-permute-done.7.a_ref, ...), custom_call_target="tpu_custom_call" | custom-call | flops 1000000000 | bytes 3000000 | tf_op jit(solution)/shard_map/grid/pallas_call | solution.py:226
  44.5 1.0 %collective-permute-start.10 = (bf16[4,4,16,128]{3,2,1,0:T(8,128)(2,1)}, bf16[4,4,16,128]{3,2,1,0:T(8,128)(2,1)S(1)}, u32[]{:S(2)}, u32[]{:S(2)}) collective-permute-start(bf16[4,4,16,128]{3,2,1,0:T(8,128)(2,1)} %get-tuple-element.19), channel_id=1, source_target_pairs={{0,2},{1,3},{2,0},{3,1},{4,6},{5,7},{6,4},{7,5},{8,10},{9,11},{10,... | collective-permute-start | bytes 196616 | tf_op jit(solution)/shard_map/ppermute | solution.py:240
  45.5 0.7 %collective-permute-start.11 = (bf16[4,4,16,128]{3,2,1,0:T(8,128)(2,1)}, bf16[4,4,16,128]{3,2,1,0:T(8,128)(2,1)S(1)}, u32[]{:S(2)}, u32[]{:S(2)}) collective-permute-start(bf16[4,4,16,128]{3,2,1,0:T(8,128)(2,1)} %get-tuple-element.20), channel_id=1, source_target_pairs={{0,3},{1,0},{2,1},{3,2},{4,7},{5,4},{6,5},{7,6},{8,11},{9,8},{10,9... | collective-permute-start | bytes 196616 | tf_op jit(solution)/shard_map/ppermute | solution.py:240
  46.2 1.4 %collective-permute-start.9 = (bf16[4,4,16,128]{3,2,1,0:T(8,128)(2,1)}, bf16[4,4,16,128]{3,2,1,0:T(8,128)(2,1)S(1)}, u32[]{:S(2)}, u32[]{:S(2)}) collective-permute-start(bf16[4,4,16,128]{3,2,1,0:T(8,128)(2,1)} %get-tuple-element.18), channel_id=1, source_target_pairs={{0,1},{1,2},{2,3},{3,0},{4,5},{5,6},{6,7},{7,4},{8,9},{9,10},{10,1... | collective-permute-start | bytes 196616 | tf_op jit(solution)/shard_map/ppermute | solution.py:240
  48.2 2.6 %time.2 = bf16[4,4,2,32,128]{4,3,2,1,0:T(8,128)(2,1)} custom-call(s32[1]{0:T(128)} %bitcast.me_ref, bf16[4,128,64]{2,1,0:T(8,128)(2,1)} %constant.32.clone.w1_ref, f32[2,32,128]{2,1,0:T(8,128)} %constant.33.clone.tw_ref, bf16[512,256]{1,0:T(8,128)(2,1)} %constant.34.clone.w2_ref, bf16[4,4,16,128]{3,2,1,0:T(8,128)(2,1)} %get-tuple-element.13.refs_0_, ...), custom_call_target="tpu_custom_call" | custom-call | flops 1000000000 | bytes 2000000 | tf_op jit(solution)/shard_map/time/pallas_call | solution.py:244
  50.8 1.0 %stack.9 = bf16[4,4,1,2,4096]{4,3,1,0,2:T(2,128)(2,1)S(1)} reshape(bf16[4,4,2,32,128]{4,3,2,1,0:T(8,128)(2,1)} %time.2) | data formatting | bytes 524288 | tf_op jit(solution)/shard_map/stack | solution.py:254
  52.5 2.6 %time.3 = bf16[4,4,2,32,128]{4,3,2,1,0:T(8,128)(2,1)} custom-call(s32[1]{0:T(128)} %bitcast.me_ref, bf16[4,128,64]{2,1,0:T(8,128)(2,1)} %constant.32.clone.w1_ref, f32[2,32,128]{2,1,0:T(8,128)} %constant.33.clone.tw_ref, bf16[512,256]{1,0:T(8,128)(2,1)} %constant.34.clone.w2_ref, bf16[4,4,16,128]{3,2,1,0:T(8,128)(2,1)} %get-tuple-element.17.refs_0_, ...), custom_call_target="tpu_custom_call" | custom-call | flops 1000000000 | bytes 2000000 | tf_op jit(solution)/shard_map/time/pallas_call | solution.py:244
  55.1 1.0 %stack.10 = bf16[4,4,1,2,4096]{4,3,1,0,2:T(2,128)(2,1)S(1)} reshape(bf16[4,4,2,32,128]{4,3,2,1,0:T(8,128)(2,1)} %time.3) | data formatting | bytes 524288 | tf_op jit(solution)/shard_map/stack | solution.py:254
  56.1 1.5 %pad_maximum_fusion.1 = bf16[4,4,2,2,4096]{4,3,2,1,0:T(2,128)(2,1)} fusion(bf16[4,4,1,2,4096]{4,3,2,1,0:T(2,128)(2,1)S(1)} %bitcast.27, bf16[4,4,1,2,4096]{4,3,2,1,0:T(2,128)(2,1)S(1)} %bitcast.26), kind=kLoop, calls=%fused_computation.3 | loop fusion | flops 262144 | bytes 1048576 | tf_op jit(solution)/shard_map/stack | solution.py:254
  (44 shorter events, 3.9 us)
Async XLA Ops:
  0.0 24.0 %collective-permute-start = (bf16[4,16,16,128]{3,2,1,0:T(8,128)(2,1)}, bf16[4,16,16,128]{3,2,1,0:T(8,128)(2,1)}, u32[]{:S(2)}, u32[]{:S(2)}) collective-permute-start(bf16[4,16,16,128]{3,2,1,0:T(8,128)(2,1)} %p_ref.1), channel_id=1, source_target_pairs={{0,4},{4,8},{8,12},{12,0},{1,5},{5,9},{9,13},{13,1},{2,6},{6,10},{... | collective-permute-start | bytes 786440 | tf_op jit(solution)/shard_map/ppermute | solution.py:177
  2.1 25.2 %collective-permute-start.1 = (bf16[4,16,16,128]{3,2,1,0:T(8,128)(2,1)}, bf16[4,16,16,128]{3,2,1,0:T(8,128)(2,1)}, u32[]{:S(2)}, u32[]{:S(2)}) collective-permute-start(bf16[4,16,16,128]{3,2,1,0:T(8,128)(2,1)} %p_ref.1), channel_id=1, source_target_pairs={{4,0},{8,4},{12,8},{0,12},{5,1},{9,5},{13,9},{1,13},{6,2},{10,6},{... | collective-permute-start | bytes 786440 | tf_op jit(solution)/shard_map/ppermute | solution.py:177
  6.0 4.2 %copy-start = (bf16[4,16,4,16,128]{4,3,2,1,0:T(8,128)(2,1)S(1)}, bf16[4,16,4,16,128]{4,3,2,1,0:T(8,128)(2,1)}, u32[]{:S(2)}) copy-start(bf16[4,16,4,16,128]{4,3,2,1,0:T(8,128)(2,1)} %param.14) | copy-start | bytes 3145732
  6.0 28.0 %collective-permute-start.2 = (bf16[128,1024]{1,0:T(8,128)(2,1)S(1)}, bf16[128,1024]{1,0:T(8,128)(2,1)}, u32[]{:S(2)}, u32[]{:S(2)}) collective-permute-start(bf16[128,1024]{1,0:T(8,128)(2,1)S(1)} %bitcast.33), channel_id=1, source_target_pairs={{0,4},{4,8},{8,12},{12,0},{1,5},{5,9},{9,13},{13,1},{2,6},{6,10},{... | collective-permute-start | bytes 786440 | tf_op jit(solution)/shard_map/ppermute | solution.py:177
  6.1 27.9 %collective-permute-start.3 = (bf16[128,1024]{1,0:T(8,128)(2,1)S(1)}, bf16[128,1024]{1,0:T(8,128)(2,1)}, u32[]{:S(2)}, u32[]{:S(2)}) collective-permute-start(bf16[128,1024]{1,0:T(8,128)(2,1)S(1)} %bitcast.34), channel_id=1, source_target_pairs={{4,0},{8,4},{12,8},{0,12},{5,1},{9,5},{13,9},{1,13},{6,2},{10,6},{... | collective-permute-start | bytes 786440 | tf_op jit(solution)/shard_map/ppermute | solution.py:177
  9.3 31.5 %collective-permute-start.7 = (bf16[128,1024]{1,0:T(8,128)(2,1)S(1)}, bf16[128,1024]{1,0:T(8,128)(2,1)}, u32[]{:S(2)}, u32[]{:S(2)}) collective-permute-start(bf16[128,1024]{1,0:T(8,128)(2,1)S(1)} %bitcast.31), channel_id=1, source_target_pairs={{0,4},{4,8},{8,12},{12,0},{1,5},{5,9},{9,13},{13,1},{2,6},{6,10},{... | collective-permute-start | bytes 786440 | tf_op jit(solution)/shard_map/ppermute | solution.py:177
  10.2 0.9 %copy-start.2 = (bf16[4,16,16,128]{3,2,1,0:T(8,128)(2,1)S(1)}, bf16[4,16,16,128]{3,2,1,0:T(8,128)(2,1)}, u32[]{:S(2)}) copy-start(bf16[4,16,16,128]{3,2,1,0:T(8,128)(2,1)} %param.13) | copy-start | bytes 786436
  10.2 1.1 %copy-start.1 = (bf16[4,16,2,2,1024]{4,3,2,1,0:T(2,128)(2,1)S(1)}, bf16[4,16,2,2,1024]{4,3,2,1,0:T(2,128)(2,1)}, u32[]{:S(2)}) copy-start(bf16[4,16,2,2,1024]{4,3,2,1,0:T(2,128)(2,1)} %param.16) | copy-start | bytes 1572868
  11.1 1.5 %copy-start.3 = (s32[4,4]{1,0:T(4,128)S(1)}, s32[4,4]{1,0:T(4,128)}, u32[]{:S(2)}) copy-start(s32[4,4]{1,0:T(4,128)} %param.15) | copy-start | bytes 196
  24.1 16.7 %collective-permute-start.8 = (bf16[128,1024]{1,0:T(8,128)(2,1)S(1)}, bf16[128,1024]{1,0:T(8,128)(2,1)S(1)}, u32[]{:S(2)}, u32[]{:S(2)}) collective-permute-start(bf16[128,1024]{1,0:T(8,128)(2,1)S(1)} %bitcast.32), channel_id=1, source_target_pairs={{4,0},{8,4},{12,8},{0,12},{5,1},{9,5},{13,9},{1,13},{6,2},{10,6},{... | collective-permute-start | bytes 786440 | tf_op jit(solution)/shard_map/ppermute | solution.py:177
  37.0 9.3 %collective-permute-start.4 = (bf16[4,4,16,128]{3,2,1,0:T(8,128)(2,1)}, bf16[4,4,16,128]{3,2,1,0:T(8,128)(2,1)S(1)}, u32[]{:S(2)}, u32[]{:S(2)}) collective-permute-start(bf16[4,4,16,128]{3,2,1,0:T(8,128)(2,1)} %get-tuple-element.14), channel_id=1, source_target_pairs={{0,1},{1,2},{2,3},{3,0},{4,5},{5,6},{6,7},{7,4},{8,9},{9,10},{10,1... | collective-permute-start | bytes 196616 | tf_op jit(solution)/shard_map/ppermute | solution.py:240
  40.4 7.2 %collective-permute-start.5 = (bf16[4,4,16,128]{3,2,1,0:T(8,128)(2,1)}, bf16[4,4,16,128]{3,2,1,0:T(8,128)(2,1)S(1)}, u32[]{:S(2)}, u32[]{:S(2)}) collective-permute-start(bf16[4,4,16,128]{3,2,1,0:T(8,128)(2,1)} %get-tuple-element.15), channel_id=1, source_target_pairs={{0,2},{1,3},{2,0},{3,1},{4,6},{5,7},{6,4},{7,5},{8,10},{9,11},{10,... | collective-permute-start | bytes 196616 | tf_op jit(solution)/shard_map/ppermute | solution.py:240
  40.4 7.2 %collective-permute-start.6 = (bf16[4,4,16,128]{3,2,1,0:T(8,128)(2,1)}, bf16[4,4,16,128]{3,2,1,0:T(8,128)(2,1)S(1)}, u32[]{:S(2)}, u32[]{:S(2)}) collective-permute-start(bf16[4,4,16,128]{3,2,1,0:T(8,128)(2,1)} %get-tuple-element.16), channel_id=1, source_target_pairs={{0,3},{1,0},{2,1},{3,2},{4,7},{5,4},{6,5},{7,6},{8,11},{9,8},{10,9... | collective-permute-start | bytes 196616 | tf_op jit(solution)/shard_map/ppermute | solution.py:240
  40.8 0.7 %copy-start.4 = (bf16[128,1024]{1,0:T(8,128)(2,1)}, bf16[128,1024]{1,0:T(8,128)(2,1)S(1)}, u32[]{:S(2)}) copy-start(bf16[128,1024]{1,0:T(8,128)(2,1)S(1)} %collective-permute-done.8.b_ref) | copy-start | bytes 786436
  44.5 7.4 %collective-permute-start.10 = (bf16[4,4,16,128]{3,2,1,0:T(8,128)(2,1)}, bf16[4,4,16,128]{3,2,1,0:T(8,128)(2,1)S(1)}, u32[]{:S(2)}, u32[]{:S(2)}) collective-permute-start(bf16[4,4,16,128]{3,2,1,0:T(8,128)(2,1)} %get-tuple-element.19), channel_id=1, source_target_pairs={{0,2},{1,3},{2,0},{3,1},{4,6},{5,7},{6,4},{7,5},{8,10},{9,11},{10,... | collective-permute-start | bytes 196616 | tf_op jit(solution)/shard_map/ppermute | solution.py:240
  45.5 6.4 %collective-permute-start.11 = (bf16[4,4,16,128]{3,2,1,0:T(8,128)(2,1)}, bf16[4,4,16,128]{3,2,1,0:T(8,128)(2,1)S(1)}, u32[]{:S(2)}, u32[]{:S(2)}) collective-permute-start(bf16[4,4,16,128]{3,2,1,0:T(8,128)(2,1)} %get-tuple-element.20), channel_id=1, source_target_pairs={{0,3},{1,0},{2,1},{3,2},{4,7},{5,4},{6,5},{7,6},{8,11},{9,8},{10,9... | collective-permute-start | bytes 196616 | tf_op jit(solution)/shard_map/ppermute | solution.py:240
  46.2 1.4 %copy-start.5 = (bf16[4,4,16,128]{3,2,1,0:T(8,128)(2,1)}, bf16[4,4,16,128]{3,2,1,0:T(8,128)(2,1)S(1)}, u32[]{:S(2)}) copy-start(bf16[4,4,16,128]{3,2,1,0:T(8,128)(2,1)S(1)} %collective-permute-done.4.refs_1_) | copy-start | bytes 196612
  46.2 5.7 %collective-permute-start.9 = (bf16[4,4,16,128]{3,2,1,0:T(8,128)(2,1)}, bf16[4,4,16,128]{3,2,1,0:T(8,128)(2,1)S(1)}, u32[]{:S(2)}, u32[]{:S(2)}) collective-permute-start(bf16[4,4,16,128]{3,2,1,0:T(8,128)(2,1)} %get-tuple-element.18), channel_id=1, source_target_pairs={{0,1},{1,2},{2,3},{3,0},{4,5},{5,6},{6,7},{7,4},{8,9},{9,10},{10,1... | collective-permute-start | bytes 196616 | tf_op jit(solution)/shard_map/ppermute | solution.py:240
  47.6 0.6 %copy-start.6 = (bf16[4,4,16,128]{3,2,1,0:T(8,128)(2,1)}, bf16[4,4,16,128]{3,2,1,0:T(8,128)(2,1)S(1)}, u32[]{:S(2)}) copy-start(bf16[4,4,16,128]{3,2,1,0:T(8,128)(2,1)S(1)} %collective-permute-done.5.refs_2_) | copy-start | bytes 196612
  47.6 0.6 %copy-start.8 = (bf16[4,4,16,128]{3,2,1,0:T(8,128)(2,1)}, bf16[4,4,16,128]{3,2,1,0:T(8,128)(2,1)S(1)}, u32[]{:S(2)}) copy-start(bf16[4,4,16,128]{3,2,1,0:T(8,128)(2,1)S(1)} %collective-permute-done.6.refs_3_) | copy-start | bytes 196612
  51.9 0.6 %copy-start.7 = (bf16[4,4,16,128]{3,2,1,0:T(8,128)(2,1)}, bf16[4,4,16,128]{3,2,1,0:T(8,128)(2,1)S(1)}, u32[]{:S(2)}) copy-start(bf16[4,4,16,128]{3,2,1,0:T(8,128)(2,1)S(1)} %collective-permute-done.10.refs_2_) | copy-start | bytes 196612
  51.9 0.6 %copy-start.9 = (bf16[4,4,16,128]{3,2,1,0:T(8,128)(2,1)}, bf16[4,4,16,128]{3,2,1,0:T(8,128)(2,1)S(1)}, u32[]{:S(2)}) copy-start(bf16[4,4,16,128]{3,2,1,0:T(8,128)(2,1)S(1)} %collective-permute-done.11.refs_3_) | copy-start | bytes 196612
  51.9 0.6 %copy-start.10 = (bf16[4,4,16,128]{3,2,1,0:T(8,128)(2,1)}, bf16[4,4,16,128]{3,2,1,0:T(8,128)(2,1)S(1)}, u32[]{:S(2)}) copy-start(bf16[4,4,16,128]{3,2,1,0:T(8,128)(2,1)S(1)} %collective-permute-done.9.refs_1_) | copy-start | bytes 196612
